TPU v7x, 32 devices: a whole 2x2x4 slice. The times are simulated.
32 devices in a mesh: slab: 4 (over y, x), block: 8 (over z, core).
Axes of the slice: x: 2, y: 2, z: 4, core: 2. Of those that a mesh axis runs over, the one named last changes fastest.
Arguments:
- lanczos_vector: float32 [3, 32, 64, 256], P(None, 'slab', 'block'), may hold values from -200 to 200
- previous_vector: float32 [3, 32, 64, 256], P(None, 'slab', 'block'), may hold values from -30 to 30
- previous_beta: float32 [], replicated, may hold values from 0.3 to 1
- locked_vectors: float32 [16, 3, 32, 64, 256], P(None, None, 'slab', 'block'), may hold values from -0.0039867997 to 0.0039867997
- occupancy: int32 [4, 8, 32], P('slab', 'block'), may hold values 0 or 1
- young: float32 [32, 64, 256], P('slab', 'block'), may hold values from 0.5 to 4
- couplings: float32 [13, 3, 3], replicated, may hold values from -1 to 1, as said below
- coarse_inverse: float32 [96, 96], P(('slab', 'block')), may hold values from -45 to 165, as said below
Outputs:
- remainder: float32 [3, 32, 64, 256], P(None, 'slab', 'block')
- coefficients: float32 [2], replicated
- projections: float32 [16], replicated
Inputs may be any that keep to these rules, and one draw needn't show every extreme that they name: `couplings`: each block is symmetric and positive definite, with positive diagonal larger than the sum of its off-diagonal magnitudes. `coarse_inverse`: symmetric and positive definite.
All inputs are finite; a program needn't handle non-finite values. No bound on the sum of `occupancy` on one device may be relied on, other than what follows from the above.
Results may differ from a plain program's by a relative error of at most 0.0003.
Values sent between devices are 32-bit elements; how exact they have to be, the bound alone decides.
No kernel may reach another device: no remote copies, remote signals or barrier semaphores. Data moves between devices by JAX's collectives and lax.ppermute only.
A program may use at most 128 MiB of HBM per device.

v0:
```python
import jax
import jax.numpy as jnp
from jax import lax
from jax.sharding import PartitionSpec as P

BRICK = 8
ITERS = 3
SHIFT_MASS = 0.02
SMOOTH_WEIGHT = 0.5
VOID_DENSITY = 0.1
HIGHEST_PRECISION = lax.Precision.HIGHEST


def with_halo(block, sides, width):
    for axis, dim in sides:
        count = lax.axis_size(axis)
        forward = [(i, i + 1) for i in range(count - 1)]
        backward = [(target, source) for source, target in forward]
        low = lax.ppermute(
            lax.slice_in_dim(block, block.shape[dim] - width, None, axis=dim), axis, forward
        )
        high = lax.ppermute(lax.slice_in_dim(block, 0, width, axis=dim), axis, backward)
        block = jnp.concatenate([low, block, high], axis=dim)
    return block


def offset_list():
    offsets = []
    for step_x in (-1, 0, 1):
        for step_y in (-1, 0, 1):
            for step_z in (-1, 0, 1):
                offsets.append((step_x, step_y, step_z))
    return offsets


def pair_block(couplings, number):
    if number < 13:
        return couplings[number]
    return couplings[26 - number]


def operate_padded(vector_field, padded_weighted, padded_root, stiffness, root_stiff, couplings):
    span_x, span_y, span_z = (vector_field.shape[1], vector_field.shape[2], vector_field.shape[3])
    accumulate = jnp.zeros_like(vector_field)
    for number, (step_x, step_y, step_z) in enumerate(offset_list()):
        if number == 13:
            continue
        matrix_pair = pair_block(couplings, number)
        root_near = padded_root[
            1 + step_x : 1 + step_x + span_x,
            1 + step_y : 1 + step_y + span_y,
            1 + step_z : 1 + step_z + span_z,
        ]
        weighted_near = padded_weighted[
            :,
            1 + step_x : 1 + step_x + span_x,
            1 + step_y : 1 + step_y + span_y,
            1 + step_z : 1 + step_z + span_z,
        ]
        differ = root_near[None] * vector_field - weighted_near
        for column in range(3):
            accumulate = (
                accumulate + matrix_pair[:, column][:, None, None, None] * differ[column][None]
            )
    return SHIFT_MASS * stiffness[None] * vector_field + root_stiff[None] * accumulate


def diagonal_of(padded_root, stiffness, root_stiff, couplings):
    span_x, span_y, span_z = stiffness.shape
    accumulate = jnp.zeros((3, span_x, span_y, span_z), jnp.float32)
    for number, (step_x, step_y, step_z) in enumerate(offset_list()):
        if number == 13:
            continue
        matrix_pair = pair_block(couplings, number)
        root_near = padded_root[
            1 + step_x : 1 + step_x + span_x,
            1 + step_y : 1 + step_y + span_y,
            1 + step_z : 1 + step_z + span_z,
        ]
        accumulate = accumulate + jnp.diagonal(matrix_pair)[:, None, None, None] * root_near[None]
    return SHIFT_MASS * stiffness[None] + root_stiff[None] * accumulate


def shards(
    lanczos_vector,
    previous_vector,
    previous_beta,
    locked_vectors,
    occupancy,
    young,
    couplings,
    coarse_inverse,
):
    density = jnp.where(occupancy == 1, 1.0, VOID_DENSITY).astype(jnp.float32)
    density = jnp.repeat(jnp.repeat(jnp.repeat(density, BRICK, 0), BRICK, 1), BRICK, 2)
    stiffness = density * young
    root_stiff = jnp.sqrt(stiffness)
    root_edges = with_halo(root_stiff, (("slab", 0), ("block", 1)), 1)
    padded_root = jnp.pad(root_edges, ((0, 0), (0, 0), (1, 1)))
    diagonal = diagonal_of(padded_root, stiffness, root_stiff, couplings)
    span_x, span_y, span_z = stiffness.shape
    slab_count = lax.axis_size("slab")
    block_count = lax.axis_size("block")

    def operate(vector_field):
        edges = with_halo(root_stiff[None] * vector_field, (("slab", 1), ("block", 2)), 1)
        padded_weighted = jnp.pad(edges, ((0, 0), (0, 0), (0, 0), (1, 1)))
        return operate_padded(
            vector_field, padded_weighted, padded_root, stiffness, root_stiff, couplings
        )

    def precondition(residual):
        smooth_first = SMOOTH_WEIGHT * residual / diagonal
        remain = residual - operate(smooth_first)
        block_means = jnp.mean(remain, axis=(1, 2, 3))
        gathered = lax.all_gather(block_means, ("slab", "block"), axis=0, tiled=True)
        own_part = jnp.dot(coarse_inverse, gathered, precision=HIGHEST_PRECISION)
        second = smooth_first + own_part[:, None, None, None]
        leftover = residual - operate(second)
        return second + SMOOTH_WEIGHT * leftover / diagonal

    def paired_sums(residual, smoothed, mapped):
        return lax.psum(
            (jnp.sum(residual * smoothed), jnp.sum(mapped * smoothed)), ("slab", "block")
        )

    solution = jnp.zeros_like(lanczos_vector)
    residual = lanczos_vector
    smoothed = precondition(residual)
    mapped = operate(smoothed)
    gamma_now, delta_now = paired_sums(residual, smoothed, mapped)
    step_size = gamma_now / delta_now
    direction = smoothed
    mapped_dir = mapped
    for number in range(ITERS):
        solution = solution + step_size * direction
        residual = residual - step_size * mapped_dir
        if number + 1 < ITERS:
            smoothed = precondition(residual)
            mapped = operate(smoothed)
            gamma_next, delta_now = paired_sums(residual, smoothed, mapped)
            ratio = gamma_next / gamma_now
            step_size = gamma_next / (delta_now - ratio * gamma_next / step_size)
            direction = smoothed + ratio * direction
            mapped_dir = mapped + ratio * mapped_dir
            gamma_now = gamma_next
    inner_part, weight = lax.psum(
        (jnp.sum(lanczos_vector * solution), jnp.sum(lanczos_vector * lanczos_vector)),
        ("slab", "block"),
    )
    alpha_now = inner_part / weight
    lanczos_part = solution - alpha_now * lanczos_vector - previous_beta * previous_vector
    local_proj = jnp.einsum(
        "kcxyz,cxyz->k", locked_vectors, lanczos_part, precision=HIGHEST_PRECISION
    )
    projections = lax.psum(local_proj, ("slab", "block"))
    remainder = lanczos_part - jnp.einsum(
        "kcxyz,k->cxyz", locked_vectors, projections, precision=HIGHEST_PRECISION
    )
    square = lax.psum(jnp.sum(remainder * remainder), ("slab", "block"))
    cell_count = 3.0 * span_x * span_y * span_z * slab_count * block_count
    beta_norm = jnp.sqrt(square / cell_count)
    return (remainder, jnp.stack([alpha_now, beta_norm]), projections)


def solution(mesh):
    in_specs = (
        P(None, "slab", "block", None),
        P(None, "slab", "block", None),
        P(),
        P(None, None, "slab", "block", None),
        P("slab", "block", None),
        P("slab", "block", None),
        P(),
        P(("slab", "block"), None),
    )
    out_specs = (P(None, "slab", "block", None), P(), P())
    return jax.shard_map(shards, mesh=mesh, in_specs=in_specs, out_specs=out_specs, check_vma=False)
```

profile of v0, /device:TPU:0, one launch (start us, length us, event | category | flops | bytes accessed | tf_op | source)
XLA Modules:
  0.0 647.6 jit_solution(7884673104356321382)
XLA Ops:
  3.8 5.5 collective-permute-start
  31.5 3.0 collective-permute-start.2
  36.1 2.3 broadcast_multiply_fusion.8
  39.7 5.5 collective-permute-start.4
  48.6 3.6 collective-permute-start.6
  53.3 1.6 select_maximum_fusion.32
  60.1 1.9 subtract_reduce_fusion.2
  63.8 45.5 %all-reduce.10 = f32[96]{0:T(128)} all-reduce(f32[96]{0:T(128)} %multiply_dynamic-update-slice_fusion.2), channel_id=1, replica_groups=mesh['slab'=4,'block'=8] {'slab','block'}, use_global_device_ids=true, to_apply=%add.10 | all-reduce | flops 96 | bytes 768
  111.6 4.8 collective-permute-start.8
  116.4 1.5 collective-permute-done.8
  119.3 1.5 collective-permute-start.11
  120.8 3.3 collective-permute-done.11
  129.1 1.5 broadcast_multiply_fusion.6
  132.1 5.4 collective-permute-start.12
  137.6 1.5 collective-permute-done.12
  140.4 4.3 collective-permute-start.14
  147.7 3.2 multiply_reduce_fusion.7
  150.9 45.5 %all-reduce.16 = (f32[]{:T(128)}, f32[]{:T(128)}) all-reduce(f32[]{:T(128)} %get-tuple-element.8, f32[]{:T(128)} %get-tuple-element.7), channel_id=1, replica_groups=mesh['slab'=4,'block'=8] {'slab','block'}, use_global_device_ids=true, to_apply=%region_2.3 | all-reduce | flops 2 | bytes 16 | tf_op jit(solution)/shard_map/psum | solution.py:123
  200.5 4.8 collective-permute-start.16
  205.3 1.5 collective-permute-done.16
  208.1 3.4 collective-permute-start.18
  216.6 1.9 subtract_reduce_fusion.1
  220.2 42.9 %all-reduce.11 = f32[96]{0:T(128)} all-reduce(f32[96]{0:T(128)} %multiply_dynamic-update-slice_fusion.1), channel_id=1, replica_groups=mesh['slab'=4,'block'=8] {'slab','block'}, use_global_device_ids=true, to_apply=%add.11 | all-reduce | flops 96 | bytes 768
  265.5 4.8 collective-permute-start.20
  274.5 3.5 collective-permute-done.23
  283.0 1.5 broadcast_multiply_fusion.3
  286.1 5.4 collective-permute-start.24
  294.4 4.5 collective-permute-start.26
  301.7 3.1 multiply_reduce_fusion.5
  304.8 45.5 %all-reduce.15 = (f32[]{:T(128)}, f32[]{:T(128)}) all-reduce(f32[]{:T(128)} %get-tuple-element.6, f32[]{:T(128)} %get-tuple-element.5), channel_id=1, replica_groups=mesh['slab'=4,'block'=8] {'slab','block'}, use_global_device_ids=true, to_apply=%region_7.8 | all-reduce | flops 2 | bytes 16 | tf_op jit(solution)/shard_map/psum | solution.py:123
  357.4 4.8 collective-permute-start.28
  365.0 3.0 collective-permute-start.30
  373.5 1.9 subtract_reduce_fusion
  377.2 43.0 %all-reduce.12 = f32[96]{0:T(128)} all-reduce(f32[96]{0:T(128)} %multiply_dynamic-update-slice_fusion), channel_id=1, replica_groups=mesh['slab'=4,'block'=8] {'slab','block'}, use_global_device_ids=true, to_apply=%add.12 | all-reduce | flops 96 | bytes 768
  422.5 4.8 collective-permute-start.32
  430.2 1.5 collective-permute-start.35
  431.7 3.3 collective-permute-done.35
  440.0 1.5 broadcast_multiply_fusion
  443.1 5.4 collective-permute-start.36
  451.4 4.3 collective-permute-start.38
  458.7 2.2 multiply_reduce_fusion.3
  461.5 45.6 %all-reduce.14 = (f32[]{:T(128)}, f32[]{:T(128)}) all-reduce(f32[]{:T(128)} %multiply_reduce_fusion.4, f32[]{:T(128)} %multiply_reduce_fusion.3), channel_id=1, replica_groups=mesh['slab'=4,'block'=8] {'slab','block'}, use_global_device_ids=true, to_apply=%region_12.13 | all-reduce | flops 2 | bytes 16 | tf_op jit(solution)/shard_map/psum | solution.py:123
  510.9 2.5 multiply_reduce_fusion.1
  513.4 40.2 %all-reduce.13 = (f32[]{:T(128)}, f32[]{:T(128)}) all-reduce(f32[]{:T(128)} %get-tuple-element.4, f32[]{:T(128)} %get-tuple-element.3), channel_id=1, replica_groups=mesh['slab'=4,'block'=8] {'slab','block'}, use_global_device_ids=true, to_apply=%region_16.17 | all-reduce | flops 2 | bytes 16 | tf_op jit(solution)/shard_map/psum | solution.py:147
  556.1 5.0 fusion.4
  561.0 40.5 %psum.78 = f32[16]{0:T(128)S(1)} all-reduce(f32[16]{0:T(128)S(1)} %fusion.4), channel_id=1, replica_groups=mesh['slab'=4,'block'=8] {'slab','block'}, use_global_device_ids=true, to_apply=%region_19.20 | all-reduce | flops 16 | bytes 128 | tf_op jit(solution)/shard_map/psum | solution.py:156
  601.6 3.3 fusion
  606.2 39.7 %psum.79 = f32[]{:T(128)} all-reduce(f32[]{:T(128)} %get-tuple-element.69), channel_id=1, replica_groups=mesh['slab'=4,'block'=8] {'slab','block'}, use_global_device_ids=true, to_apply=%region_21.22 | all-reduce | flops 1 | bytes 8 | tf_op jit(solution)/shard_map/psum | solution.py:160
  (1179 shorter events, 109.2 us)
Async XLA Ops:
  0.6 555.4 %copy-start = (f32[16,3,8,8,256]{4,3,2,1,0:T(8,128)S(1)}, f32[16,3,8,8,256]{4,3,2,1,0:T(8,128)}, u32[]{:S(2)}) copy-start(f32[16,3,8,8,256]{4,3,2,1,0:T(8,128)} %param.11) | copy-start | bytes 9437188
  2.5 27.6 %collective-permute-start.1 = (f32[1,8,256]{2,1,0:T(8,128)S(1)}, f32[1,8,256]{2,1,0:T(8,128)S(1)}, u32[]{:S(2)}, u32[]{:S(2)}) collective-permute-start(f32[1,8,256]{2,1,0:T(8,128)S(1)} %get-tuple-element.1154), channel_id=1, source_target_pairs={{8,0},{16,8},{24,16},{9,1},{17,9},{25,17},{10,2},{18,10},{26,18},{... | collective-permute-start | bytes 24584 | tf_op jit(solution)/shard_map/ppermute | solution.py:22
  3.8 26.3 %collective-permute-start = (f32[1,8,256]{2,1,0:T(8,128)S(1)}, f32[1,8,256]{2,1,0:T(8,128)S(1)}, u32[]{:S(2)}, u32[]{:S(2)}) collective-permute-start(f32[1,8,256]{2,1,0:T(8,128)S(1)} %get-tuple-element.1153), channel_id=1, source_target_pairs={{0,8},{8,16},{16,24},{1,9},{9,17},{17,25},{2,10},{10,18},{18,26},{... | collective-permute-start | bytes 24584 | tf_op jit(solution)/shard_map/ppermute | solution.py:19
  30.2 4.4 collective-permute-start.3
  31.5 3.9 collective-permute-start.2
  35.7 17.3 %copy-start.5 = (f32[8,8,256]{2,1,0:T(8,128)}, f32[8,8,256]{2,1,0:T(8,128)S(1)}, u32[]{:S(2)}) copy-start(f32[8,8,256]{2,1,0:T(8,128)S(1)} %get-tuple-element.360) | copy-start | bytes 196612
  35.8 17.2 %copy-start.12 = (f32[8,8,256]{2,1,0:T(8,128)}, f32[8,8,256]{2,1,0:T(8,128)S(1)}, u32[]{:S(2)}) copy-start(f32[8,8,256]{2,1,0:T(8,128)S(1)} %get-tuple-element.361) | copy-start | bytes 196612
  35.8 17.2 %copy-start.19 = (f32[8,8,256]{2,1,0:T(8,128)}, f32[8,8,256]{2,1,0:T(8,128)S(1)}, u32[]{:S(2)}) copy-start(f32[8,8,256]{2,1,0:T(8,128)S(1)} %get-tuple-element.362) | copy-start | bytes 196612
  38.4 7.6 %collective-permute-start.5 = (f32[3,1,8,256]{3,2,1,0:T(8,128)S(1)}, f32[3,1,8,256]{3,2,1,0:T(8,128)S(1)}, u32[]{:S(2)}, u32[]{:S(2)}) collective-permute-start(f32[3,1,8,256]{3,2,1,0:T(8,128)S(1)} %get-tuple-element.1138), channel_id=1, source_target_pairs={{8,0},{16,8},{24,16},{9,1},{17,9},{25,17},{10,2},{18,10},{26,18},{... | collective-permute-start | bytes 73736 | tf_op jit(solution)/shard_map/ppermute | solution.py:22
  39.7 7.0 %collective-permute-start.4 = (f32[3,1,8,256]{3,2,1,0:T(8,128)S(1)}, f32[3,1,8,256]{3,2,1,0:T(8,128)S(1)}, u32[]{:S(2)}, u32[]{:S(2)}) collective-permute-start(f32[3,1,8,256]{3,2,1,0:T(8,128)S(1)} %get-tuple-element.1137), channel_id=1, source_target_pairs={{0,8},{8,16},{16,24},{1,9},{9,17},{17,25},{2,10},{10,18},{18,26},{... | collective-permute-start | bytes 73736 | tf_op jit(solution)/shard_map/ppermute | solution.py:19
  47.3 6.0 collective-permute-start.7
  48.6 4.7 collective-permute-start.6
  110.3 6.1 collective-permute-start.9
  111.6 6.3 collective-permute-start.8
  118.0 2.8 collective-permute-start.10
  119.3 4.8 collective-permute-start.11
  130.7 6.9 %collective-permute-start.13 = (f32[3,1,8,256]{3,2,1,0:T(8,128)S(1)}, f32[3,1,8,256]{3,2,1,0:T(8,128)S(1)}, u32[]{:S(2)}, u32[]{:S(2)}) collective-permute-start(f32[3,1,8,256]{3,2,1,0:T(8,128)S(1)} %get-tuple-element.973), channel_id=1, source_target_pairs={{8,0},{16,8},{24,16},{9,1},{17,9},{25,17},{10,2},{18,10},{26,18},{... | collective-permute-start | bytes 73736 | tf_op jit(solution)/shard_map/ppermute | solution.py:22
  132.1 7.0 %collective-permute-start.12 = (f32[3,1,8,256]{3,2,1,0:T(8,128)S(1)}, f32[3,1,8,256]{3,2,1,0:T(8,128)S(1)}, u32[]{:S(2)}, u32[]{:S(2)}) collective-permute-start(f32[3,1,8,256]{3,2,1,0:T(8,128)S(1)} %get-tuple-element.972), channel_id=1, source_target_pairs={{0,8},{8,16},{16,24},{1,9},{9,17},{17,25},{2,10},{10,18},{18,26},{... | collective-permute-start | bytes 73736 | tf_op jit(solution)/shard_map/ppermute | solution.py:19
  139.1 5.6 collective-permute-start.15
  140.4 5.1 collective-permute-start.14
  198.9 17.3 %copy-start.160 = (f32[3,8,8,256]{3,2,1,0:T(8,128)}, f32[3,8,8,256]{3,2,1,0:T(8,128)S(1)}, u32[]{:S(2)}) copy-start(f32[3,8,8,256]{3,2,1,0:T(8,128)S(1)} %get-tuple-element.82) | copy-start | bytes 589828
  199.0 6.3 collective-permute-start.17
  200.5 6.3 collective-permute-start.16
  206.8 4.7 collective-permute-start.19
  208.1 3.9 collective-permute-start.18
  264.2 6.1 collective-permute-start.21
  265.5 6.3 collective-permute-start.20
  271.9 2.6 collective-permute-start.22
  273.2 4.9 collective-permute-start.23
  284.7 6.9 %collective-permute-start.25 = (f32[3,1,8,256]{3,2,1,0:T(8,128)S(1)}, f32[3,1,8,256]{3,2,1,0:T(8,128)S(1)}, u32[]{:S(2)}, u32[]{:S(2)}) collective-permute-start(f32[3,1,8,256]{3,2,1,0:T(8,128)S(1)} %get-tuple-element.723), channel_id=1, source_target_pairs={{8,0},{16,8},{24,16},{9,1},{17,9},{25,17},{10,2},{18,10},{26,18},{... | collective-permute-start | bytes 73736 | tf_op jit(solution)/shard_map/ppermute | solution.py:22
  286.1 7.0 %collective-permute-start.24 = (f32[3,1,8,256]{3,2,1,0:T(8,128)S(1)}, f32[3,1,8,256]{3,2,1,0:T(8,128)S(1)}, u32[]{:S(2)}, u32[]{:S(2)}) collective-permute-start(f32[3,1,8,256]{3,2,1,0:T(8,128)S(1)} %get-tuple-element.722), channel_id=1, source_target_pairs={{0,8},{8,16},{16,24},{1,9},{9,17},{17,25},{2,10},{10,18},{18,26},{... | collective-permute-start | bytes 73736 | tf_op jit(solution)/shard_map/ppermute | solution.py:19
  293.1 5.8 collective-permute-start.27
  294.4 5.1 collective-permute-start.26
  355.8 17.3 %copy-start.162 = (f32[3,8,8,256]{3,2,1,0:T(8,128)}, f32[3,8,8,256]{3,2,1,0:T(8,128)S(1)}, u32[]{:S(2)}) copy-start(f32[3,8,8,256]{3,2,1,0:T(8,128)S(1)} %get-tuple-element.76) | copy-start | bytes 589828
  355.9 6.3 collective-permute-start.29
  357.4 6.3 collective-permute-start.28
  363.7 4.3 collective-permute-start.31
  365.0 3.9 collective-permute-start.30
  421.2 6.1 collective-permute-start.33
  422.5 6.3 collective-permute-start.32
  428.9 2.8 collective-permute-start.34
  430.2 4.9 collective-permute-start.35
  441.7 6.9 %collective-permute-start.37 = (f32[3,1,8,256]{3,2,1,0:T(8,128)S(1)}, f32[3,1,8,256]{3,2,1,0:T(8,128)S(1)}, u32[]{:S(2)}, u32[]{:S(2)}) collective-permute-start(f32[3,1,8,256]{3,2,1,0:T(8,128)S(1)} %get-tuple-element.473), channel_id=1, source_target_pairs={{8,0},{16,8},{24,16},{9,1},{17,9},{25,17},{10,2},{18,10},{26,18},{... | collective-permute-start | bytes 73736 | tf_op jit(solution)/shard_map/ppermute | solution.py:22
  443.1 7.0 %collective-permute-start.36 = (f32[3,1,8,256]{3,2,1,0:T(8,128)S(1)}, f32[3,1,8,256]{3,2,1,0:T(8,128)S(1)}, u32[]{:S(2)}, u32[]{:S(2)}) collective-permute-start(f32[3,1,8,256]{3,2,1,0:T(8,128)S(1)} %get-tuple-element.472), channel_id=1, source_target_pairs={{0,8},{8,16},{16,24},{1,9},{9,17},{17,25},{2,10},{10,18},{18,26},{... | collective-permute-start | bytes 73736 | tf_op jit(solution)/shard_map/ppermute | solution.py:19
  450.1 6.3 collective-permute-start.39
  451.4 5.1 collective-permute-start.38
  458.6 52.3 %copy-start.4 = (f32[3,8,8,256]{3,2,1,0:T(8,128)S(1)}, f32[3,8,8,256]{3,2,1,0:T(8,128)}, u32[]{:S(2)}) copy-start(f32[3,8,8,256]{3,2,1,0:T(8,128)} %param.8) | copy-start | bytes 589828
  601.6 45.6 %copy-start.386 = (f32[16]{0:T(128)}, f32[16]{0:T(128)S(1)}, u32[]{:S(2)}) copy-start(f32[16]{0:T(128)S(1)} %psum.78) | copy-start | bytes 196
  (379 other events, 1714.3 us)
where the time goes:
time: 658 us; the launch traced here: 648 us
  blocking collectives  388 us (59%)
  starting transfers between devices  108 us (16%)
  other arithmetic  58.5 us (9%)
  local copies, waits for them, and re-layouts  33.5 us (5%)
  waiting for transfers between devices  26.5 us (4%)
  between operations  21.4 us (3%)
  matrix products  11 us (2%)
    psum x3, blocking collectives, paired_sums(): lax.psum((jnp.sum(residual * smoothed), jnp.sum(mapped * smoothed)), ('sl...  137 us
    unnamed x3, blocking collectives  131 us
    ppermute x20, starting transfers between devices, with_halo(): lax.ppermute(lax.slice_in_dim(block, block.shape[dim] - width, None, axis...  81.4 us
    psum x1, blocking collectives, shards(): projections = lax.psum(local_proj, ('slab', 'block'))  40.5 us
    psum x1, blocking collectives, shards(): lax.psum((jnp.sum(lanczos_vector * solution), jnp.sum(lanczos_vector * la...  40.2 us
    psum x1, blocking collectives, shards(): square = lax.psum(jnp.sum(remainder * remainder), ('slab', 'block'))  39.7 us
    ppermute x20, starting transfers between devices, with_halo(): lax.ppermute(lax.slice_in_dim(block, 0, width, axis=dim), axis, backward)  26.9 us
    ppermute x20, waiting for transfers between devices, with_halo(): lax.ppermute(lax.slice_in_dim(block, block.shape[dim] - width, None, axis...  16.3 us
  transfers between devices with their start and end apart: 40, of which 18 were waited for; matrix products, arithmetic and copies ran while one was open for 4% of the time, Pallas kernels for 0%

commit v1 on v0

--- a/solution.py
+++ b/solution.py
@@ -2,6 +2,7 @@
 import jax.numpy as jnp
 from jax import lax
 from jax.sharding import PartitionSpec as P
+from jax.lax import psum
 
 BRICK = 8
 ITERS = 3
@@ -144,9 +145,12 @@
             direction = smoothed + ratio * direction
             mapped_dir = mapped + ratio * mapped_dir
             gamma_now = gamma_next
-    inner_part, weight = lax.psum(
-        (jnp.sum(lanczos_vector * solution), jnp.sum(lanczos_vector * lanczos_vector)),
-        ("slab", "block"),
+    inner_part, weight = psum(
+        psum(
+            (jnp.sum(lanczos_vector * solution), jnp.sum(lanczos_vector * lanczos_vector)),
+            axis_name="slab",
+        ),
+        axis_name="block",
     )
     alpha_now = inner_part / weight
     lanczos_part = solution - alpha_now * lanczos_vector - previous_beta * previous_vector

time: 658 us -> 642 us (0.976)
  blocking collectives: 388 us -> 372 us
    psum x1 -> x2, blocking collectives: 40.2 us -> 25.7 us  [the longest x1 14.5 us: shards(): psum(psum((jnp.sum(lanczos_vector * solution), jnp.sum(lanczos_vector * l...]
where the time goes in v1:
time: 642 us; the launch traced here: 632 us
  blocking collectives  372 us (58%)
  starting transfers between devices  108 us (17%)
  other arithmetic  58.5 us (9%)
  local copies, waits for them, and re-layouts  33.5 us (5%)
  waiting for transfers between devices  26.5 us (4%)
  between operations  21.8 us (3%)
  matrix products  11 us (2%)
    psum x3, blocking collectives, paired_sums(): lax.psum((jnp.sum(residual * smoothed), jnp.sum(mapped * smoothed)), ('sl...  137 us
    unnamed x3, blocking collectives  131 us
    ppermute x20, starting transfers between devices, with_halo(): lax.ppermute(lax.slice_in_dim(block, block.shape[dim] - width, None, axis...  81.4 us
    psum x1, blocking collectives, shards(): square = lax.psum(jnp.sum(remainder * remainder), ('slab', 'block'))  41.6 us
    psum x1, blocking collectives, shards(): projections = lax.psum(local_proj, ('slab', 'block'))  36.8 us
    ppermute x20, starting transfers between devices, with_halo(): lax.ppermute(lax.slice_in_dim(block, 0, width, axis=dim), axis, backward)  26.9 us
    ppermute x20, waiting for transfers between devices, with_halo(): lax.ppermute(lax.slice_in_dim(block, block.shape[dim] - width, None, axis...  16.3 us
    gather x13, local copies, waits for them, and re-layouts, diagonal_of(): jnp.diagonal(matrix_pair)[:, None, None, None] * root_near[None]  15.3 us
  transfers between devices with their start and end apart: 40, of which 18 were waited for; matrix products, arithmetic and copies ran while one was open for 4% of the time, Pallas kernels for 0%

profile of v1, /device:TPU:0, one launch (start us, length us, event | category | flops | bytes accessed | tf_op | source)
XLA Modules:
  0.0 631.7 jit_solution(13906522380621562511)
XLA Ops:
  3.8 5.5 collective-permute-start
  31.4 3.0 collective-permute-start.2
  36.1 2.3 broadcast_multiply_fusion.8
  39.6 5.5 collective-permute-start.4
  48.6 3.6 collective-permute-start.6
  53.3 1.6 select_maximum_fusion.32
  60.1 1.9 subtract_reduce_fusion.2
  63.8 45.5 %all-reduce.10 = f32[96]{0:T(128)} all-reduce(f32[96]{0:T(128)} %multiply_dynamic-update-slice_fusion.2), channel_id=1, replica_groups=mesh['slab'=4,'block'=8] {'slab','block'}, use_global_device_ids=true, to_apply=%add.10 | all-reduce | flops 96 | bytes 768
  111.6 4.8 collective-permute-start.8
  116.4 1.5 collective-permute-done.8
  119.2 1.5 collective-permute-start.11
  120.8 3.3 collective-permute-done.11
  129.1 1.5 broadcast_multiply_fusion.6
  132.1 5.4 collective-permute-start.12
  140.4 4.3 collective-permute-start.14
  147.7 3.2 multiply_reduce_fusion.7
  150.9 45.5 %all-reduce.15 = (f32[]{:T(128)}, f32[]{:T(128)}) all-reduce(f32[]{:T(128)} %get-tuple-element.8, f32[]{:T(128)} %get-tuple-element.7), channel_id=1, replica_groups=mesh['slab'=4,'block'=8] {'slab','block'}, use_global_device_ids=true, to_apply=%region_2.3 | all-reduce | flops 2 | bytes 16 | tf_op jit(solution)/shard_map/psum | solution.py:124
  200.5 4.8 collective-permute-start.16
  208.1 3.4 collective-permute-start.18
  216.6 1.9 subtract_reduce_fusion.1
  220.3 43.0 %all-reduce.11 = f32[96]{0:T(128)} all-reduce(f32[96]{0:T(128)} %multiply_dynamic-update-slice_fusion.1), channel_id=1, replica_groups=mesh['slab'=4,'block'=8] {'slab','block'}, use_global_device_ids=true, to_apply=%add.11 | all-reduce | flops 96 | bytes 768
  265.6 4.8 collective-permute-start.20
  270.4 1.5 collective-permute-done.20
  274.6 3.5 collective-permute-done.23
  283.1 1.5 broadcast_multiply_fusion.3
  286.2 5.4 collective-permute-start.24
  294.5 4.5 collective-permute-start.26
  301.8 3.1 multiply_reduce_fusion.5
  304.9 45.5 %all-reduce.14 = (f32[]{:T(128)}, f32[]{:T(128)}) all-reduce(f32[]{:T(128)} %get-tuple-element.6, f32[]{:T(128)} %get-tuple-element.5), channel_id=1, replica_groups=mesh['slab'=4,'block'=8] {'slab','block'}, use_global_device_ids=true, to_apply=%region_7.8 | all-reduce | flops 2 | bytes 16 | tf_op jit(solution)/shard_map/psum | solution.py:124
  357.7 4.8 collective-permute-start.28
  365.3 3.0 collective-permute-start.30
  373.8 1.9 subtract_reduce_fusion
  377.5 43.0 %all-reduce.12 = f32[96]{0:T(128)} all-reduce(f32[96]{0:T(128)} %multiply_dynamic-update-slice_fusion), channel_id=1, replica_groups=mesh['slab'=4,'block'=8] {'slab','block'}, use_global_device_ids=true, to_apply=%add.12 | all-reduce | flops 96 | bytes 768
  422.8 4.8 collective-permute-start.32
  430.5 1.5 collective-permute-start.35
  432.0 3.3 collective-permute-done.35
  440.4 1.5 broadcast_multiply_fusion
  443.4 5.4 collective-permute-start.36
  451.7 4.3 collective-permute-start.38
  459.0 2.2 multiply_reduce_fusion.3
  461.8 45.6 %all-reduce.13 = (f32[]{:T(128)}, f32[]{:T(128)}) all-reduce(f32[]{:T(128)} %multiply_reduce_fusion.4, f32[]{:T(128)} %multiply_reduce_fusion.3), channel_id=1, replica_groups=mesh['slab'=4,'block'=8] {'slab','block'}, use_global_device_ids=true, to_apply=%region_12.13 | all-reduce | flops 2 | bytes 16 | tf_op jit(solution)/shard_map/psum | solution.py:124
  511.4 2.5 multiply_reduce_fusion.1
  513.9 11.2 %all-reduce.17 = (f32[]{:T(128)}, f32[]{:T(128)}) all-reduce(f32[]{:T(128)} %get-tuple-element.4, f32[]{:T(128)} %get-tuple-element.3), channel_id=1, replica_groups=mesh['slab'=4,'block'=8] {'slab'}, use_global_device_ids=true, to_apply=%region_16.17 | all-reduce | flops 2 | bytes 16 | tf_op jit(solution)/shard_map/psum | solution.py:149
  525.1 14.5 %all-reduce.16 = (f32[]{:T(128)}, f32[]{:T(128)}) all-reduce(f32[]{:T(128)} %get-tuple-element.69, f32[]{:T(128)} %get-tuple-element.70), channel_id=1, replica_groups=mesh['slab'=4,'block'=8] {'block'}, use_global_device_ids=true, to_apply=%region_17.18 | all-reduce | flops 2 | bytes 16 | tf_op jit(solution)/shard_map/psum | solution.py:148
  541.9 5.0 fusion.4
  546.9 36.8 %psum.94 = f32[16]{0:T(128)S(1)} all-reduce(f32[16]{0:T(128)S(1)} %fusion.4), channel_id=1, replica_groups=mesh['slab'=4,'block'=8] {'slab','block'}, use_global_device_ids=true, to_apply=%region_21.22 | all-reduce | flops 16 | bytes 128 | tf_op jit(solution)/shard_map/psum | solution.py:160
  583.7 3.3 fusion
  588.3 41.6 %psum.95 = f32[]{:T(128)} all-reduce(f32[]{:T(128)} %get-tuple-element.71), channel_id=1, replica_groups=mesh['slab'=4,'block'=8] {'slab','block'}, use_global_device_ids=true, to_apply=%region_23.24 | all-reduce | flops 1 | bytes 8 | tf_op jit(solution)/shard_map/psum | solution.py:164
  (1180 shorter events, 110.7 us)
Async XLA Ops:
  0.6 541.3 %copy-start = (f32[16,3,8,8,256]{4,3,2,1,0:T(8,128)S(1)}, f32[16,3,8,8,256]{4,3,2,1,0:T(8,128)}, u32[]{:S(2)}) copy-start(f32[16,3,8,8,256]{4,3,2,1,0:T(8,128)} %param.11) | copy-start | bytes 9437188
  2.5 27.6 %collective-permute-start.1 = (f32[1,8,256]{2,1,0:T(8,128)S(1)}, f32[1,8,256]{2,1,0:T(8,128)S(1)}, u32[]{:S(2)}, u32[]{:S(2)}) collective-permute-start(f32[1,8,256]{2,1,0:T(8,128)S(1)} %get-tuple-element.1156), channel_id=1, source_target_pairs={{8,0},{16,8},{24,16},{9,1},{17,9},{25,17},{10,2},{18,10},{26,18},{... | collective-permute-start | bytes 24584 | tf_op jit(solution)/shard_map/ppermute | solution.py:23
  3.8 26.3 %collective-permute-start = (f32[1,8,256]{2,1,0:T(8,128)S(1)}, f32[1,8,256]{2,1,0:T(8,128)S(1)}, u32[]{:S(2)}, u32[]{:S(2)}) collective-permute-start(f32[1,8,256]{2,1,0:T(8,128)S(1)} %get-tuple-element.1155), channel_id=1, source_target_pairs={{0,8},{8,16},{16,24},{1,9},{9,17},{17,25},{2,10},{10,18},{18,26},{... | collective-permute-start | bytes 24584 | tf_op jit(solution)/shard_map/ppermute | solution.py:20
  30.1 4.4 collective-permute-start.3
  31.4 3.9 collective-permute-start.2
  35.7 17.3 %copy-start.5 = (f32[8,8,256]{2,1,0:T(8,128)}, f32[8,8,256]{2,1,0:T(8,128)S(1)}, u32[]{:S(2)}) copy-start(f32[8,8,256]{2,1,0:T(8,128)S(1)} %get-tuple-element.362) | copy-start | bytes 196612
  35.7 17.3 %copy-start.12 = (f32[8,8,256]{2,1,0:T(8,128)}, f32[8,8,256]{2,1,0:T(8,128)S(1)}, u32[]{:S(2)}) copy-start(f32[8,8,256]{2,1,0:T(8,128)S(1)} %get-tuple-element.363) | copy-start | bytes 196612
  35.7 17.3 %copy-start.19 = (f32[8,8,256]{2,1,0:T(8,128)}, f32[8,8,256]{2,1,0:T(8,128)S(1)}, u32[]{:S(2)}) copy-start(f32[8,8,256]{2,1,0:T(8,128)S(1)} %get-tuple-element.364) | copy-start | bytes 196612
  38.3 7.6 %collective-permute-start.5 = (f32[3,1,8,256]{3,2,1,0:T(8,128)S(1)}, f32[3,1,8,256]{3,2,1,0:T(8,128)S(1)}, u32[]{:S(2)}, u32[]{:S(2)}) collective-permute-start(f32[3,1,8,256]{3,2,1,0:T(8,128)S(1)} %get-tuple-element.1140), channel_id=1, source_target_pairs={{8,0},{16,8},{24,16},{9,1},{17,9},{25,17},{10,2},{18,10},{26,18},{... | collective-permute-start | bytes 73736 | tf_op jit(solution)/shard_map/ppermute | solution.py:23
  39.6 7.0 %collective-permute-start.4 = (f32[3,1,8,256]{3,2,1,0:T(8,128)S(1)}, f32[3,1,8,256]{3,2,1,0:T(8,128)S(1)}, u32[]{:S(2)}, u32[]{:S(2)}) collective-permute-start(f32[3,1,8,256]{3,2,1,0:T(8,128)S(1)} %get-tuple-element.1139), channel_id=1, source_target_pairs={{0,8},{8,16},{16,24},{1,9},{9,17},{17,25},{2,10},{10,18},{18,26},{... | collective-permute-start | bytes 73736 | tf_op jit(solution)/shard_map/ppermute | solution.py:20
  47.3 6.0 collective-permute-start.7
  48.6 4.7 collective-permute-start.6
  110.3 6.1 collective-permute-start.9
  111.6 6.3 collective-permute-start.8
  117.9 2.8 collective-permute-start.10
  119.2 4.8 collective-permute-start.11
  130.7 6.9 %collective-permute-start.13 = (f32[3,1,8,256]{3,2,1,0:T(8,128)S(1)}, f32[3,1,8,256]{3,2,1,0:T(8,128)S(1)}, u32[]{:S(2)}, u32[]{:S(2)}) collective-permute-start(f32[3,1,8,256]{3,2,1,0:T(8,128)S(1)} %get-tuple-element.975), channel_id=1, source_target_pairs={{8,0},{16,8},{24,16},{9,1},{17,9},{25,17},{10,2},{18,10},{26,18},{... | collective-permute-start | bytes 73736 | tf_op jit(solution)/shard_map/ppermute | solution.py:23
  132.1 7.0 %collective-permute-start.12 = (f32[3,1,8,256]{3,2,1,0:T(8,128)S(1)}, f32[3,1,8,256]{3,2,1,0:T(8,128)S(1)}, u32[]{:S(2)}, u32[]{:S(2)}) collective-permute-start(f32[3,1,8,256]{3,2,1,0:T(8,128)S(1)} %get-tuple-element.974), channel_id=1, source_target_pairs={{0,8},{8,16},{16,24},{1,9},{9,17},{17,25},{2,10},{10,18},{18,26},{... | collective-permute-start | bytes 73736 | tf_op jit(solution)/shard_map/ppermute | solution.py:20
  139.1 5.6 collective-permute-start.15
  140.4 5.1 collective-permute-start.14
  198.9 17.3 %copy-start.160 = (f32[3,8,8,256]{3,2,1,0:T(8,128)}, f32[3,8,8,256]{3,2,1,0:T(8,128)S(1)}, u32[]{:S(2)}) copy-start(f32[3,8,8,256]{3,2,1,0:T(8,128)S(1)} %get-tuple-element.84) | copy-start | bytes 589828
  199.0 6.3 collective-permute-start.17
  200.5 6.3 %collective-permute-start.16 = (f32[3,1,8,256]{3,2,1,0:T(8,128)S(1)}, f32[3,1,8,256]{3,2,1,0:T(8,128)S(1)}, u32[]{:S(2)}, u32[]{:S(2)}) collective-permute-start(f32[3,1,8,256]{3,2,1,0:T(8,128)S(1)} %get-tuple-element.889), channel_id=1, source_target_pairs={{0,8},{8,16},{16,24},{1,9},{9,17},{17,25},{2,10},{10,18},{18,26},{... | collective-permute-start | bytes 73736 | tf_op jit(solution)/shard_map/ppermute | solution.py:20
  206.8 4.7 collective-permute-start.19
  208.1 3.9 collective-permute-start.18
  264.3 6.1 collective-permute-start.21
  265.6 6.3 collective-permute-start.20
  272.0 2.6 collective-permute-start.22
  273.3 4.9 collective-permute-start.23
  284.7 6.9 %collective-permute-start.25 = (f32[3,1,8,256]{3,2,1,0:T(8,128)S(1)}, f32[3,1,8,256]{3,2,1,0:T(8,128)S(1)}, u32[]{:S(2)}, u32[]{:S(2)}) collective-permute-start(f32[3,1,8,256]{3,2,1,0:T(8,128)S(1)} %get-tuple-element.725), channel_id=1, source_target_pairs={{8,0},{16,8},{24,16},{9,1},{17,9},{25,17},{10,2},{18,10},{26,18},{... | collective-permute-start | bytes 73736 | tf_op jit(solution)/shard_map/ppermute | solution.py:23
  286.2 7.0 %collective-permute-start.24 = (f32[3,1,8,256]{3,2,1,0:T(8,128)S(1)}, f32[3,1,8,256]{3,2,1,0:T(8,128)S(1)}, u32[]{:S(2)}, u32[]{:S(2)}) collective-permute-start(f32[3,1,8,256]{3,2,1,0:T(8,128)S(1)} %get-tuple-element.724), channel_id=1, source_target_pairs={{0,8},{8,16},{16,24},{1,9},{9,17},{17,25},{2,10},{10,18},{18,26},{... | collective-permute-start | bytes 73736 | tf_op jit(solution)/shard_map/ppermute | solution.py:20
  293.2 5.8 collective-permute-start.27
  294.5 5.1 collective-permute-start.26
  356.1 17.3 %copy-start.162 = (f32[3,8,8,256]{3,2,1,0:T(8,128)}, f32[3,8,8,256]{3,2,1,0:T(8,128)S(1)}, u32[]{:S(2)}) copy-start(f32[3,8,8,256]{3,2,1,0:T(8,128)S(1)} %get-tuple-element.78) | copy-start | bytes 589828
  356.2 6.3 collective-permute-start.29
  357.7 6.3 %collective-permute-start.28 = (f32[3,1,8,256]{3,2,1,0:T(8,128)S(1)}, f32[3,1,8,256]{3,2,1,0:T(8,128)S(1)}, u32[]{:S(2)}, u32[]{:S(2)}) collective-permute-start(f32[3,1,8,256]{3,2,1,0:T(8,128)S(1)} %get-tuple-element.639), channel_id=1, source_target_pairs={{0,8},{8,16},{16,24},{1,9},{9,17},{17,25},{2,10},{10,18},{18,26},{... | collective-permute-start | bytes 73736 | tf_op jit(solution)/shard_map/ppermute | solution.py:20
  364.0 4.3 collective-permute-start.31
  365.3 3.9 collective-permute-start.30
  421.5 6.1 collective-permute-start.33
  422.8 6.3 collective-permute-start.32
  429.2 2.8 collective-permute-start.34
  430.5 4.9 collective-permute-start.35
  442.0 6.9 %collective-permute-start.37 = (f32[3,1,8,256]{3,2,1,0:T(8,128)S(1)}, f32[3,1,8,256]{3,2,1,0:T(8,128)S(1)}, u32[]{:S(2)}, u32[]{:S(2)}) collective-permute-start(f32[3,1,8,256]{3,2,1,0:T(8,128)S(1)} %get-tuple-element.475), channel_id=1, source_target_pairs={{8,0},{16,8},{24,16},{9,1},{17,9},{25,17},{10,2},{18,10},{26,18},{... | collective-permute-start | bytes 73736 | tf_op jit(solution)/shard_map/ppermute | solution.py:23
  443.4 7.0 %collective-permute-start.36 = (f32[3,1,8,256]{3,2,1,0:T(8,128)S(1)}, f32[3,1,8,256]{3,2,1,0:T(8,128)S(1)}, u32[]{:S(2)}, u32[]{:S(2)}) collective-permute-start(f32[3,1,8,256]{3,2,1,0:T(8,128)S(1)} %get-tuple-element.474), channel_id=1, source_target_pairs={{0,8},{8,16},{16,24},{1,9},{9,17},{17,25},{2,10},{10,18},{18,26},{... | collective-permute-start | bytes 73736 | tf_op jit(solution)/shard_map/ppermute | solution.py:20
  450.4 6.3 collective-permute-start.39
  451.7 5.1 collective-permute-start.38
  458.9 52.4 %copy-start.4 = (f32[3,8,8,256]{3,2,1,0:T(8,128)S(1)}, f32[3,8,8,256]{3,2,1,0:T(8,128)}, u32[]{:S(2)}) copy-start(f32[3,8,8,256]{3,2,1,0:T(8,128)} %param.8) | copy-start | bytes 589828
  583.7 47.5 %copy-start.386 = (f32[16]{0:T(128)}, f32[16]{0:T(128)S(1)}, u32[]{:S(2)}) copy-start(f32[16]{0:T(128)S(1)} %psum.94) | copy-start | bytes 196
  (379 other events, 1715.2 us)
